TPU v7x, 128 devices: a whole 4x4x4 slice. The times are simulated.
128 devices in a mesh: req: 32 (over x, z, core), mlp: 4 (over y).
Axes of the slice: x: 4, y: 4, z: 4, core: 2. Of those that a mesh axis runs over, the one named last changes fastest.
Arguments:
- queries: bfloat16 [16896, 2048], P('req', 'mlp'), may hold values from -6 to 6
- key_cache: bfloat16 [2560, 128, 1024], P('req', None, 'mlp'), may hold values from -6 to 6
- value_cache: bfloat16 [2560, 128, 1024], P('req', None, 'mlp'), may hold values from -6 to 6
- decode_len: int32 [512], P('req'), may hold values from 1 to 4096, as said below
- stretch_start: int32 [32], P('req'), may hold values from 0 to 3584, as said below
- page_table: int32 [544, 32], P('req'), may hold values from 0 to 79, as said below
- hidden_in: bfloat16 [16896, 2304], P('req')
- o_weight: bfloat16 [2048, 2304], P('mlp'), may hold values from -0.125 to 0.125
- attn_gain: float32 [2304], replicated, may hold values from 0.1 to 1.9
- ffn_in_gain: float32 [2304], replicated, may hold values from 0.1 to 1.9
- ffn_out_gain: float32 [2304], replicated, may hold values from 0.1 to 1.9
- w_gate: bfloat16 [2304, 9216], P('req', 'mlp'), may hold values from -0.125 to 0.125
- w_up: bfloat16 [2304, 9216], P('req', 'mlp'), may hold values from -0.125 to 0.125
- w_down: bfloat16 [2304, 9216], P('req', 'mlp')
Outputs:
- layer_out: bfloat16 [16896, 2304], P('req', 'mlp')
Inputs may be any that keep to these rules, and one draw needn't show every extreme that they name: `decode_len`: each decode request's tokens fill its first pages; request 1 of req index 1 holds 4096 tokens. `stretch_start`: req index 0 starts at 3584, req index 1 at 0. `page_table`: row j of req index r's block of 17 rows names request j's pages by slot in that index's own pool of 80 pages; the slots holding a req index's tokens are all distinct; entries past a request's last page are valid slots that hold none of its tokens.
All inputs are finite; a program needn't handle non-finite values.
Results may differ from a plain program's by a relative error of at most 0.014.
Values may be sent and summed in bfloat16 or wider, within the bound.
A program may use at most 128 MiB of HBM per device.

v0:
```python
import math
import jax
import jax.numpy as jnp
from jax import lax
from jax.sharding import PartitionSpec as P

H = 8
KVH = 4
HD = 256
PRE_DEV = 512
DEC_DEV = 16
EPS = 1e-06
CAP = 50.0


def rms(values, gain):
    return values * lax.rsqrt(jnp.mean(values * values, axis=-1, keepdims=True) + EPS) * gain


def capped_weight(scores, visible):
    capped = CAP * jnp.tanh(scores / (16.0 * CAP))
    return jnp.where(visible, jnp.exp(capped), jnp.float32(0.0))


def attend(queries, key_cache, value_cache, decode_len, stretch_start, page_table):
    rows = queries.shape[0]
    local_kv = key_cache.shape[2] // HD
    rep = H // KVH
    page_len = key_cache.shape[1]
    max_pages = page_table.shape[1]
    requests = page_table.shape[0]
    block = math.gcd(max_pages, max(1, 512 // page_len))
    span = block * page_len
    query = queries.reshape(rows, local_kv, rep, HD)
    pre_q = query[:PRE_DEV]
    dec_q = query[PRE_DEV:]
    start = stretch_start[0]
    limit = start + jnp.arange(PRE_DEV, dtype=jnp.int32) + 1
    need = jnp.maximum(
        (start + PRE_DEV + page_len - 1) // page_len,
        jnp.max((decode_len + page_len - 1) // page_len),
    )
    blocks = (need + block - 1) // block

    def step(index, carry):
        pre_num, pre_den, dec_num, dec_den = carry
        slots = lax.dynamic_slice_in_dim(page_table, index * block, block, 1)
        keys = key_cache[slots].reshape(requests, span, local_kv, HD)
        vals = value_cache[slots].reshape(requests, span, local_kv, HD)
        position = index * span + jnp.arange(span, dtype=jnp.int32)
        pre_scores = jnp.einsum(
            "rghd,tgd->rght", pre_q, keys[0], preferred_element_type=jnp.float32
        )
        pre_weight = capped_weight(
            pre_scores, position[None, None, None, :] < limit[:, None, None, None]
        )
        pre_num = pre_num + jnp.einsum(
            "rght,tgd->rghd",
            pre_weight.astype(jnp.bfloat16),
            vals[0],
            preferred_element_type=jnp.float32,
        )
        pre_den = pre_den + jnp.sum(pre_weight, axis=-1)
        dec_scores = jnp.einsum(
            "rghd,rtgd->rght", dec_q, keys[1:], preferred_element_type=jnp.float32
        )
        dec_weight = capped_weight(
            dec_scores, position[None, None, None, :] < decode_len[:, None, None, None]
        )
        dec_num = dec_num + jnp.einsum(
            "rght,rtgd->rghd",
            dec_weight.astype(jnp.bfloat16),
            vals[1:],
            preferred_element_type=jnp.float32,
        )
        dec_den = dec_den + jnp.sum(dec_weight, axis=-1)
        return (pre_num, pre_den, dec_num, dec_den)

    start_carry = (
        jnp.zeros((PRE_DEV, local_kv, rep, HD), jnp.float32),
        jnp.zeros((PRE_DEV, local_kv, rep), jnp.float32),
        jnp.zeros((DEC_DEV, local_kv, rep, HD), jnp.float32),
        jnp.zeros((DEC_DEV, local_kv, rep), jnp.float32),
    )
    pre_num, pre_den, dec_num, dec_den = lax.fori_loop(0, blocks, step, start_carry)
    pre_out = (pre_num / pre_den[..., None]).astype(jnp.bfloat16)
    dec_out = (dec_num / dec_den[..., None]).astype(jnp.bfloat16)
    return jnp.concatenate([pre_out, dec_out], axis=0).reshape(rows, local_kv * rep * HD)


def per_device(
    queries,
    key_cache,
    value_cache,
    decode_len,
    stretch_start,
    page_table,
    hidden_in,
    o_weight,
    attn_gain,
    ffn_in_gain,
    ffn_out_gain,
    w_gate,
    w_up,
    w_down,
):
    attended = attend(queries, key_cache, value_cache, decode_len, stretch_start, page_table)
    projected = lax.psum(
        jnp.dot(attended, o_weight, preferred_element_type=jnp.float32).astype(jnp.bfloat16), "mlp"
    ).astype(jnp.float32)
    resid = hidden_in.astype(jnp.float32) + rms(projected, attn_gain)
    normed = rms(resid, ffn_in_gain).astype(jnp.bfloat16)
    gate = jnp.dot(
        normed,
        lax.all_gather(w_gate, "req", axis=0, tiled=True),
        preferred_element_type=jnp.float32,
    )
    up_part = jnp.dot(
        normed, lax.all_gather(w_up, "req", axis=0, tiled=True), preferred_element_type=jnp.float32
    )
    act = (jax.nn.gelu(gate, approximate=True) * up_part).astype(jnp.bfloat16)
    partial_out = lax.dot_general(
        act,
        lax.all_gather(w_down, "req", axis=0, tiled=True),
        (((1,), (1,)), ((), ())),
        preferred_element_type=jnp.float32,
    )
    width = hidden_in.shape[1] // lax.axis_size("mlp")
    first = lax.axis_index("mlp") * width
    total = lax.psum(partial_out.astype(jnp.bfloat16), "mlp").astype(jnp.float32)
    combined = resid + rms(total, ffn_out_gain)
    result = lax.dynamic_slice_in_dim(combined, first, width, 1)
    return result.astype(jnp.bfloat16)


def solution(mesh):
    return jax.shard_map(
        per_device,
        mesh=mesh,
        in_specs=(
            P("req", "mlp"),
            P("req", None, "mlp"),
            P("req", None, "mlp"),
            P("req"),
            P("req"),
            P("req", None),
            P("req", None),
            P("mlp", None),
            P(),
            P(),
            P(),
            P("req", "mlp"),
            P("req", "mlp"),
            P("req", "mlp"),
        ),
        out_specs=P("req", "mlp"),
        check_vma=False,
    )
```

profile of v0, /device:TPU:1, one launch (start us, length us, event | category | flops | bytes accessed | tf_op | source)
XLA Modules:
  0.0 542.8 jit_solution(7240394064184673819)
XLA Ops:
  13.4 251.5 %while.17 = (s32[]{:T(128)}, f32[512,1,2,256]{0,3,2,1:T(8,128)S(1)}, f32[512,1,2]{0,2,1:T(2,128)S(1)}, f32[16,1,2,256]{3,2,0,1:T(2,128)S(1)}, f32[16,1,2]{0,2,1:...) while((s32[]{:T(128)}, ...), condition=%wide.region_4.5_spmd.clone, body=%wide.region_1.4_spmd.clone.sunk | while | flops 556894976 | bytes 58393828 | solution.py:85
  14.3 7.9 %gather_fusion.1 = bf16[68,128,256]{2,1,0:T(8,128)(2,1)} fusion(bf16[80,128,256]{2,1,0:T(8,128)(2,1)} %get-tuple-element.310, s32[1024]{0:T(1024)S(1)} %pad_clamp_fusion.2), kind=kCustom, calls=%fused_computation.1.clone.clone.1 | custom fusion | bytes 8913168 | tf_op jit(solution)/shard_map/while/body/gather | solution.py:48
  24.7 3.0 fusion.59
  27.7 7.9 %gather_fusion = bf16[68,128,256]{2,1,0:T(8,128)(2,1)} fusion(bf16[80,128,256]{2,1,0:T(8,128)(2,1)} %get-tuple-element.309, s32[1024]{0:T(1024)S(1)} %pad_clamp_fusion.2), kind=kCustom, calls=%fused_computation.clone.clone.1 | custom fusion | bytes 8913168 | tf_op jit(solution)/shard_map/while/body/gather | solution.py:49
  41.8 2.2 slice-done.1
  45.7 7.9 %gather_fusion.1 = bf16[68,128,256]{2,1,0:T(8,128)(2,1)} fusion(bf16[80,128,256]{2,1,0:T(8,128)(2,1)} %get-tuple-element.310, s32[1024]{0:T(1024)S(1)} %pad_clamp_fusion.2), kind=kCustom, calls=%fused_computation.1.clone.clone.1 | custom fusion | bytes 8913168 | tf_op jit(solution)/shard_map/while/body/gather | solution.py:48
  56.1 3.0 fusion.59
  59.2 7.9 %gather_fusion = bf16[68,128,256]{2,1,0:T(8,128)(2,1)} fusion(bf16[80,128,256]{2,1,0:T(8,128)(2,1)} %get-tuple-element.309, s32[1024]{0:T(1024)S(1)} %pad_clamp_fusion.2), kind=kCustom, calls=%fused_computation.clone.clone.1 | custom fusion | bytes 8913168 | tf_op jit(solution)/shard_map/while/body/gather | solution.py:49
  73.3 2.2 slice-done.1
  77.1 7.9 %gather_fusion.1 = bf16[68,128,256]{2,1,0:T(8,128)(2,1)} fusion(bf16[80,128,256]{2,1,0:T(8,128)(2,1)} %get-tuple-element.310, s32[1024]{0:T(1024)S(1)} %pad_clamp_fusion.2), kind=kCustom, calls=%fused_computation.1.clone.clone.1 | custom fusion | bytes 8913168 | tf_op jit(solution)/shard_map/while/body/gather | solution.py:48
  87.6 3.0 fusion.59
  90.6 7.9 %gather_fusion = bf16[68,128,256]{2,1,0:T(8,128)(2,1)} fusion(bf16[80,128,256]{2,1,0:T(8,128)(2,1)} %get-tuple-element.309, s32[1024]{0:T(1024)S(1)} %pad_clamp_fusion.2), kind=kCustom, calls=%fused_computation.clone.clone.1 | custom fusion | bytes 8913168 | tf_op jit(solution)/shard_map/while/body/gather | solution.py:49
  104.7 2.2 slice-done.1
  108.6 7.9 %gather_fusion.1 = bf16[68,128,256]{2,1,0:T(8,128)(2,1)} fusion(bf16[80,128,256]{2,1,0:T(8,128)(2,1)} %get-tuple-element.310, s32[1024]{0:T(1024)S(1)} %pad_clamp_fusion.2), kind=kCustom, calls=%fused_computation.1.clone.clone.1 | custom fusion | bytes 8913168 | tf_op jit(solution)/shard_map/while/body/gather | solution.py:48
  119.0 3.0 fusion.59
  122.0 7.9 %gather_fusion = bf16[68,128,256]{2,1,0:T(8,128)(2,1)} fusion(bf16[80,128,256]{2,1,0:T(8,128)(2,1)} %get-tuple-element.309, s32[1024]{0:T(1024)S(1)} %pad_clamp_fusion.2), kind=kCustom, calls=%fused_computation.clone.clone.1 | custom fusion | bytes 8913168 | tf_op jit(solution)/shard_map/while/body/gather | solution.py:49
  136.2 2.2 slice-done.1
  140.0 7.9 %gather_fusion.1 = bf16[68,128,256]{2,1,0:T(8,128)(2,1)} fusion(bf16[80,128,256]{2,1,0:T(8,128)(2,1)} %get-tuple-element.310, s32[1024]{0:T(1024)S(1)} %pad_clamp_fusion.2), kind=kCustom, calls=%fused_computation.1.clone.clone.1 | custom fusion | bytes 8913168 | tf_op jit(solution)/shard_map/while/body/gather | solution.py:48
  150.4 3.0 fusion.59
  153.5 7.9 %gather_fusion = bf16[68,128,256]{2,1,0:T(8,128)(2,1)} fusion(bf16[80,128,256]{2,1,0:T(8,128)(2,1)} %get-tuple-element.309, s32[1024]{0:T(1024)S(1)} %pad_clamp_fusion.2), kind=kCustom, calls=%fused_computation.clone.clone.1 | custom fusion | bytes 8913168 | tf_op jit(solution)/shard_map/while/body/gather | solution.py:49
  167.6 2.2 slice-done.1
  171.4 7.9 %gather_fusion.1 = bf16[68,128,256]{2,1,0:T(8,128)(2,1)} fusion(bf16[80,128,256]{2,1,0:T(8,128)(2,1)} %get-tuple-element.310, s32[1024]{0:T(1024)S(1)} %pad_clamp_fusion.2), kind=kCustom, calls=%fused_computation.1.clone.clone.1 | custom fusion | bytes 8913168 | tf_op jit(solution)/shard_map/while/body/gather | solution.py:48
  181.9 3.0 fusion.59
  184.9 7.9 %gather_fusion = bf16[68,128,256]{2,1,0:T(8,128)(2,1)} fusion(bf16[80,128,256]{2,1,0:T(8,128)(2,1)} %get-tuple-element.309, s32[1024]{0:T(1024)S(1)} %pad_clamp_fusion.2), kind=kCustom, calls=%fused_computation.clone.clone.1 | custom fusion | bytes 8913168 | tf_op jit(solution)/shard_map/while/body/gather | solution.py:49
  193.8 1.7 fusion.60
  199.0 2.2 slice-done.1
  202.9 7.9 %gather_fusion.1 = bf16[68,128,256]{2,1,0:T(8,128)(2,1)} fusion(bf16[80,128,256]{2,1,0:T(8,128)(2,1)} %get-tuple-element.310, s32[1024]{0:T(1024)S(1)} %pad_clamp_fusion.2), kind=kCustom, calls=%fused_computation.1.clone.clone.1 | custom fusion | bytes 8913168 | tf_op jit(solution)/shard_map/while/body/gather | solution.py:48
  213.3 3.0 fusion.59
  216.4 7.9 %gather_fusion = bf16[68,128,256]{2,1,0:T(8,128)(2,1)} fusion(bf16[80,128,256]{2,1,0:T(8,128)(2,1)} %get-tuple-element.309, s32[1024]{0:T(1024)S(1)} %pad_clamp_fusion.2), kind=kCustom, calls=%fused_computation.clone.clone.1 | custom fusion | bytes 8913168 | tf_op jit(solution)/shard_map/while/body/gather | solution.py:49
  230.5 2.2 slice-done.1
  234.3 7.9 %gather_fusion.1 = bf16[68,128,256]{2,1,0:T(8,128)(2,1)} fusion(bf16[80,128,256]{2,1,0:T(8,128)(2,1)} %get-tuple-element.310, s32[1024]{0:T(1024)S(1)} %pad_clamp_fusion.2), kind=kCustom, calls=%fused_computation.1.clone.clone.1 | custom fusion | bytes 8913168 | tf_op jit(solution)/shard_map/while/body/gather | solution.py:48
  244.7 3.0 fusion.59
  247.8 7.9 %gather_fusion = bf16[68,128,256]{2,1,0:T(8,128)(2,1)} fusion(bf16[80,128,256]{2,1,0:T(8,128)(2,1)} %get-tuple-element.309, s32[1024]{0:T(1024)S(1)} %pad_clamp_fusion.2), kind=kCustom, calls=%fused_computation.clone.clone.1 | custom fusion | bytes 8913168 | tf_op jit(solution)/shard_map/while/body/gather | solution.py:49
  256.7 1.7 fusion.60
  261.9 2.2 slice-done.1
  266.7 2.9 convolution_convert_fusion.1
  271.6 64.7 %all-reduce.3.cloned.1.call-done = bf16[528,2304]{1,0:T(8,128)(2,1)} async-done(((bf16[528,2304]{1,0:T(8,128)(2,1)}), bf16[528,2304]{1,0:T(8,128)(2,1)}) %all-reduce.3.cloned.1.call-update) | async-done | bytes 2433040 | tf_op jit(solution)/shard_map/psum | solution.py:108
  336.3 2.2 fusion.14
  338.6 5.8 %multiply_reduce_fusion.1 = (f32[528]{0:T(1024)S(1)}, f32[528,2304]{1,0:T(8,128)}) fusion(f32[2304]{0:T(1024)S(1)} %copy-done.3, f32[528]{0:T(1024)S(1)} %add_rsqrt_fusion.2, bf16[528,2304]{1,0:T(8,128)(2,1)} %all-reduce.3.cloned.1.call-done, bf16[528,2304]{1,0:T(8,128)(2,1)} %param.22), kind=kLoop, calls=%fused_computation.43 | loop fusion | flops 8515056 | bytes 9745536 | tf_op jit(solution)/shard_map/reduce_sum | solution.py:17
  344.4 12.5 %fusion.28 = f32[528,2304]{1,0:T(8,128)} fusion(bf16[2304,2304]{1,0:T(8,128)(2,1)} %all-gather.4.cloned.1.call-done, f32[528,2304]{1,0:T(8,128)} %get-tuple-element.163, f32[2304]{0:T(1024)S(1)} %copy-done.4, f32[528]{0:T(1024)S(1)} %add_rsqrt_fusion.1), kind=kOutput, calls=%fused_computation.62 | convolution fusion | flops 5609336832 | bytes 20360256 | tf_op jit(solution)/shard_map/dot_general | solution.py:113
  356.9 36.1 %all-gather.6.cloned.1.call-done = bf16[2304,2304]{1,0:T(8,128)(2,1)} async-done(((bf16[72,2304]{1,0:T(8,128)(2,1)}), bf16[2304,2304]{1,0:T(8,128)(2,1)}) %all-gather.6.cloned.1.call-update) | async-done | bytes 10616848 | tf_op jit(solution)/shard_map/all_gather | solution.py:119
  393.0 12.9 %fusion.24 = bf16[528,2304]{1,0:T(8,128)(2,1)} fusion(bf16[2304,2304]{1,0:T(8,128)(2,1)} %all-gather.6.cloned.1.call-done, f32[528,2304]{1,0:T(8,128)} %fusion.28, f32[528,2304]{1,0:T(8,128)} %get-tuple-element.163, f32[2304]{0:T(1024)S(1)} %copy-done.4, f32[528]{0:T(1024)S(1)} %add_rsqrt_fusion.1), kind=kOutput, calls=%fused_computation.44 | convolution fusion | flops 5621501952 | bytes 22793280 | tf_op jit(solution)/shard_map/dot_general | solution.py:118
  405.8 46.8 %all-gather.8.cloned.1.call-done = bf16[2304,2304]{1,0:T(8,128)(2,1)} async-done(((bf16[72,2304]{1,0:T(8,128)(2,1)}), bf16[2304,2304]{1,0:T(8,128)(2,1)}) %all-gather.8.cloned.1.call-update) | async-done | bytes 10616848 | tf_op jit(solution)/shard_map/all_gather | solution.py:124
  452.7 11.6 %convolution_convert_fusion = bf16[528,2304]{1,0:T(8,128)(2,1)} fusion(bf16[528,2304]{1,0:T(8,128)(2,1)} %fusion.24, bf16[2304,2304]{1,0:T(8,128)(2,1)} %all-gather.8.cloned.1.call-done), kind=kOutput, calls=%fused_computation.45 | convolution fusion | flops 5606903808 | bytes 15482880 | tf_op jit(solution)/shard_map/dot_general | solution.py:122
  465.1 62.5 %all-reduce.5.cloned.1.call-done = bf16[528,2304]{1,0:T(8,128)(2,1)} async-done(((bf16[528,2304]{1,0:T(8,128)(2,1)}), bf16[528,2304]{1,0:T(8,128)(2,1)}) %all-reduce.5.cloned.1.call-update) | async-done | bytes 2433040 | tf_op jit(solution)/shard_map/psum | solution.py:130
  527.6 2.2 multiply_reduce_fusion
  529.9 2.2 convert_element_type.45
  532.1 3.2 fusion.25
  (188 shorter events, 88.3 us)
Async XLA Ops:
  7.4 259.3 %copy-start = (bf16[512,2304]{1,0:T(8,128)(2,1)S(1)}, bf16[512,2304]{1,0:T(8,128)(2,1)}, u32[]{:S(2)}) copy-start(bf16[512,2304]{1,0:T(8,128)(2,1)} %param.23) | copy-start | bytes 7077892
  7.4 329.0 %all-reduce.3.cloned.1.call-start = ((), (), s32[]{:S(2)}) async-start(), calls=%async_computation | async-start | bytes 4866048 | tf_op jit(solution)/shard_map/psum | solution.py:108
  38.4 0.7 copy-start.2
  38.4 2.2 slice-start
  41.8 2.2 slice-start.1
  69.8 0.7 copy-start.2
  69.8 2.2 slice-start
  73.3 2.2 slice-start.1
  101.2 0.7 copy-start.2
  101.2 2.2 slice-start
  104.7 2.2 slice-start.1
  132.7 0.7 copy-start.2
  132.7 2.2 slice-start
  136.2 2.2 slice-start.1
  164.1 0.7 copy-start.2
  164.1 2.2 slice-start
  167.6 2.2 slice-start.1
  195.5 0.7 copy-start.2
  195.5 2.2 slice-start
  199.0 2.2 slice-start.1
  227.0 0.7 copy-start.2
  227.0 2.2 slice-start
  230.5 2.2 slice-start.1
  258.4 0.7 copy-start.2
  258.4 2.2 slice-start
  261.9 2.2 slice-start.1
  269.6 69.0 %copy-start.3 = (f32[2304]{0:T(1024)S(1)}, f32[2304]{0:T(1024)}, u32[]{:S(2)}) copy-start(f32[2304]{0:T(1024)} %param.24) | copy-start | bytes 27652
  269.6 74.8 %all-gather.4.cloned.1.call-start = ((), (), s32[]{:S(2)}) async-start(), calls=%async_computation.1 | async-start | bytes 10948608 | tf_op jit(solution)/shard_map/all_gather | solution.py:115
  270.2 122.7 %all-gather.6.cloned.1.call-start = ((), (), s32[]{:S(2)}) async-start(), calls=%async_computation.2 | async-start | bytes 10948608 | tf_op jit(solution)/shard_map/all_gather | solution.py:119
  270.8 181.9 %all-gather.8.cloned.1.call-start = ((), (), s32[]{:S(2)}) async-start(), calls=%async_computation.3 | async-start | bytes 10948608 | tf_op jit(solution)/shard_map/all_gather | solution.py:124
  271.4 256.2 %all-reduce.5.cloned.1.call-start = ((), (), s32[]{:S(2)}) async-start(), calls=%async_computation.4 | async-start | bytes 4866048 | tf_op jit(solution)/shard_map/psum | solution.py:130
  338.6 5.8 %copy-start.4 = (f32[2304]{0:T(1024)S(1)}, f32[2304]{0:T(1024)}, u32[]{:S(2)}) copy-start(f32[2304]{0:T(1024)} %param.25) | copy-start | bytes 27652
  529.8 5.4 copy-start.1
Sparse Core Ops, SparseCore 0:
  269.8 66.5 all-reduce.2
  464.4 63.1 all-reduce.4
Sparse Core Ops, SparseCore 1:
  272.5 60.8 all-gather.3
  335.5 57.4 all-gather.5
  395.2 57.4 all-gather.7
where the time goes:
time: 546 us; the launch traced here: 543 us
  waiting for transfers between devices  212 us (39%)
  local copies, waits for them, and re-layouts  188 us (34%)
  matrix products  93.3 us (17%)
  other arithmetic  31.8 us (6%)
  between operations  16.6 us (3%)
    psum x1, waiting for transfers between devices, per_device(): lax.psum(jnp.dot(attended, o_weight, preferred_element_type=jnp.float32)....  64.7 us
    gather x8, local copies, waits for them, and re-layouts, step(): vals = value_cache[slots].reshape(requests, span, local_kv, HD)  63.5 us
    gather x8, local copies, waits for them, and re-layouts, step(): keys = key_cache[slots].reshape(requests, span, local_kv, HD)  62.9 us
    psum x1, waiting for transfers between devices, per_device(): lax.psum(partial_out.astype(jnp.bfloat16), 'mlp').astype(jnp.float32)  62.5 us
    all_gather x1, waiting for transfers between devices, per_device(): lax.all_gather(w_down, 'req', axis=0, tiled=True)  46.8 us
    all_gather x1, waiting for transfers between devices, per_device(): lax.all_gather(w_up, 'req', axis=0, tiled=True)  36.1 us
    dot_general x8, matrix products, step(): jnp.einsum('rghd,tgd->rght', pre_q, keys[0], preferred_element_type=jnp.f...  24.4 us
    slice x16, local copies, waits for them, and re-layouts, step(): vals[1:]  17.6 us
  transfers between devices with their start and end apart: 5, of which 4 were waited for; matrix products, arithmetic and copies ran while one was open for 6% of the time, Pallas kernels for 0%

commit v1 on v0

--- a/solution.py
+++ b/solution.py
@@ -121,7 +121,9 @@
     act = (jax.nn.gelu(gate, approximate=True) * up_part).astype(jnp.bfloat16)
     partial_out = lax.dot_general(
         act,
-        lax.all_gather(w_down, "req", axis=0, tiled=True),
+        jnp.concatenate(
+            lax.all_to_all(jnp.stack([w_down] * lax.axis_size("req")), "req", 0, 0), axis=0
+        ),
         (((1,), (1,)), ((), ())),
         preferred_element_type=jnp.float32,
     )

time: 546 us -> 606 us (1.11)
  waiting for transfers between devices: 212 us -> 259 us
  starting transfers between devices: 0.35 us -> 9.11 us
    all_gather x1, waiting for transfers between devices: 0.01 us -> 88.9 us  [per_device(): lax.all_gather(w_gate, 'req', axis=0, tiled=True)]
    all_gather x1 -> x0, waiting for transfers between devices: 46.8 us -> none  [per_device(): lax.all_gather(w_down, 'req', axis=0, tiled=True)]
    all_gather x1, waiting for transfers between devices: 36.1 us -> 54.7 us  [per_device(): lax.all_gather(w_up, 'req', axis=0, tiled=True)]
    psum x1, waiting for transfers between devices: 64.7 us -> 51.9 us  [per_device(): lax.psum(jnp.dot(attended, o_weight, preferred_element_type=jnp.float32)....]
    all_to_all x0 -> x1, starting transfers between devices: none -> 8.8 us  [per_device(): lax.all_to_all(jnp.stack([w_down] * lax.axis_size('req')), 'req', 0, 0)]
where the time goes in v1:
time: 606 us; the launch traced here: 603 us
  waiting for transfers between devices  259 us (43%)
  local copies, waits for them, and re-layouts  193 us (32%)
  matrix products  93.1 us (15%)
  other arithmetic  31.9 us (5%)
  between operations  16.5 us (3%)
  starting transfers between devices  9.11 us (2%)
    all_gather x1, waiting for transfers between devices, per_device(): lax.all_gather(w_gate, 'req', axis=0, tiled=True)  88.9 us
    gather x8, local copies, waits for them, and re-layouts, step(): vals = value_cache[slots].reshape(requests, span, local_kv, HD)  63.5 us
    gather x8, local copies, waits for them, and re-layouts, step(): keys = key_cache[slots].reshape(requests, span, local_kv, HD)  62.9 us
    psum x1, waiting for transfers between devices, per_device(): lax.psum(partial_out.astype(jnp.bfloat16), 'mlp').astype(jnp.float32)  62.5 us
    all_gather x1, waiting for transfers between devices, per_device(): lax.all_gather(w_up, 'req', axis=0, tiled=True)  54.7 us
    psum x1, waiting for transfers between devices, per_device(): lax.psum(jnp.dot(attended, o_weight, preferred_element_type=jnp.float32)....  51.9 us
    dot_general x8, matrix products, step(): jnp.einsum('rghd,tgd->rght', pre_q, keys[0], preferred_element_type=jnp.f...  24.4 us
    slice x16, local copies, waits for them, and re-layouts, step(): vals[1:]  17.6 us
  transfers between devices with their start and end apart: 5, of which 4 were waited for; matrix products, arithmetic and copies ran while one was open for 6% of the time, Pallas kernels for 0%

profile of v1, /device:TPU:1, one launch (start us, length us, event | category | flops | bytes accessed | tf_op | source)
XLA Modules:
  0.0 603.3 jit_solution(13582177318966095978)
XLA Ops:
  13.4 251.5 %while.17 = (s32[]{:T(128)}, f32[512,1,2,256]{0,3,2,1:T(8,128)S(1)}, f32[512,1,2]{0,2,1:T(2,128)S(1)}, f32[16,1,2,256]{3,2,0,1:T(2,128)S(1)}, f32[16,1,2]{0,2,1:...) while((s32[]{:T(128)}, ...), condition=%wide.region_4.5_spmd.clone, body=%wide.region_1.4_spmd.clone.sunk | while | flops 556894976 | bytes 58393828 | solution.py:85
  14.3 7.9 %gather_fusion.1 = bf16[68,128,256]{2,1,0:T(8,128)(2,1)} fusion(bf16[80,128,256]{2,1,0:T(8,128)(2,1)} %get-tuple-element.310, s32[1024]{0:T(1024)S(1)} %pad_clamp_fusion.2), kind=kCustom, calls=%fused_computation.1.clone.clone.1 | custom fusion | bytes 8913168 | tf_op jit(solution)/shard_map/while/body/gather | solution.py:48
  24.7 3.0 fusion.59
  27.7 7.9 %gather_fusion = bf16[68,128,256]{2,1,0:T(8,128)(2,1)} fusion(bf16[80,128,256]{2,1,0:T(8,128)(2,1)} %get-tuple-element.309, s32[1024]{0:T(1024)S(1)} %pad_clamp_fusion.2), kind=kCustom, calls=%fused_computation.clone.clone.1 | custom fusion | bytes 8913168 | tf_op jit(solution)/shard_map/while/body/gather | solution.py:49
  41.8 2.2 slice-done.1
  45.7 7.9 %gather_fusion.1 = bf16[68,128,256]{2,1,0:T(8,128)(2,1)} fusion(bf16[80,128,256]{2,1,0:T(8,128)(2,1)} %get-tuple-element.310, s32[1024]{0:T(1024)S(1)} %pad_clamp_fusion.2), kind=kCustom, calls=%fused_computation.1.clone.clone.1 | custom fusion | bytes 8913168 | tf_op jit(solution)/shard_map/while/body/gather | solution.py:48
  56.1 3.0 fusion.59
  59.2 7.9 %gather_fusion = bf16[68,128,256]{2,1,0:T(8,128)(2,1)} fusion(bf16[80,128,256]{2,1,0:T(8,128)(2,1)} %get-tuple-element.309, s32[1024]{0:T(1024)S(1)} %pad_clamp_fusion.2), kind=kCustom, calls=%fused_computation.clone.clone.1 | custom fusion | bytes 8913168 | tf_op jit(solution)/shard_map/while/body/gather | solution.py:49
  73.3 2.2 slice-done.1
  77.1 7.9 %gather_fusion.1 = bf16[68,128,256]{2,1,0:T(8,128)(2,1)} fusion(bf16[80,128,256]{2,1,0:T(8,128)(2,1)} %get-tuple-element.310, s32[1024]{0:T(1024)S(1)} %pad_clamp_fusion.2), kind=kCustom, calls=%fused_computation.1.clone.clone.1 | custom fusion | bytes 8913168 | tf_op jit(solution)/shard_map/while/body/gather | solution.py:48
  87.6 3.0 fusion.59
  90.6 7.9 %gather_fusion = bf16[68,128,256]{2,1,0:T(8,128)(2,1)} fusion(bf16[80,128,256]{2,1,0:T(8,128)(2,1)} %get-tuple-element.309, s32[1024]{0:T(1024)S(1)} %pad_clamp_fusion.2), kind=kCustom, calls=%fused_computation.clone.clone.1 | custom fusion | bytes 8913168 | tf_op jit(solution)/shard_map/while/body/gather | solution.py:49
  104.7 2.2 slice-done.1
  108.6 7.9 %gather_fusion.1 = bf16[68,128,256]{2,1,0:T(8,128)(2,1)} fusion(bf16[80,128,256]{2,1,0:T(8,128)(2,1)} %get-tuple-element.310, s32[1024]{0:T(1024)S(1)} %pad_clamp_fusion.2), kind=kCustom, calls=%fused_computation.1.clone.clone.1 | custom fusion | bytes 8913168 | tf_op jit(solution)/shard_map/while/body/gather | solution.py:48
  119.0 3.0 fusion.59
  122.0 7.9 %gather_fusion = bf16[68,128,256]{2,1,0:T(8,128)(2,1)} fusion(bf16[80,128,256]{2,1,0:T(8,128)(2,1)} %get-tuple-element.309, s32[1024]{0:T(1024)S(1)} %pad_clamp_fusion.2), kind=kCustom, calls=%fused_computation.clone.clone.1 | custom fusion | bytes 8913168 | tf_op jit(solution)/shard_map/while/body/gather | solution.py:49
  136.2 2.2 slice-done.1
  140.0 7.9 %gather_fusion.1 = bf16[68,128,256]{2,1,0:T(8,128)(2,1)} fusion(bf16[80,128,256]{2,1,0:T(8,128)(2,1)} %get-tuple-element.310, s32[1024]{0:T(1024)S(1)} %pad_clamp_fusion.2), kind=kCustom, calls=%fused_computation.1.clone.clone.1 | custom fusion | bytes 8913168 | tf_op jit(solution)/shard_map/while/body/gather | solution.py:48
  150.4 3.0 fusion.59
  153.5 7.9 %gather_fusion = bf16[68,128,256]{2,1,0:T(8,128)(2,1)} fusion(bf16[80,128,256]{2,1,0:T(8,128)(2,1)} %get-tuple-element.309, s32[1024]{0:T(1024)S(1)} %pad_clamp_fusion.2), kind=kCustom, calls=%fused_computation.clone.clone.1 | custom fusion | bytes 8913168 | tf_op jit(solution)/shard_map/while/body/gather | solution.py:49
  167.6 2.2 slice-done.1
  171.4 7.9 %gather_fusion.1 = bf16[68,128,256]{2,1,0:T(8,128)(2,1)} fusion(bf16[80,128,256]{2,1,0:T(8,128)(2,1)} %get-tuple-element.310, s32[1024]{0:T(1024)S(1)} %pad_clamp_fusion.2), kind=kCustom, calls=%fused_computation.1.clone.clone.1 | custom fusion | bytes 8913168 | tf_op jit(solution)/shard_map/while/body/gather | solution.py:48
  181.9 3.0 fusion.59
  184.9 7.9 %gather_fusion = bf16[68,128,256]{2,1,0:T(8,128)(2,1)} fusion(bf16[80,128,256]{2,1,0:T(8,128)(2,1)} %get-tuple-element.309, s32[1024]{0:T(1024)S(1)} %pad_clamp_fusion.2), kind=kCustom, calls=%fused_computation.clone.clone.1 | custom fusion | bytes 8913168 | tf_op jit(solution)/shard_map/while/body/gather | solution.py:49
  199.0 2.2 slice-done.1
  202.9 7.9 %gather_fusion.1 = bf16[68,128,256]{2,1,0:T(8,128)(2,1)} fusion(bf16[80,128,256]{2,1,0:T(8,128)(2,1)} %get-tuple-element.310, s32[1024]{0:T(1024)S(1)} %pad_clamp_fusion.2), kind=kCustom, calls=%fused_computation.1.clone.clone.1 | custom fusion | bytes 8913168 | tf_op jit(solution)/shard_map/while/body/gather | solution.py:48
  213.3 3.0 fusion.59
  216.4 7.9 %gather_fusion = bf16[68,128,256]{2,1,0:T(8,128)(2,1)} fusion(bf16[80,128,256]{2,1,0:T(8,128)(2,1)} %get-tuple-element.309, s32[1024]{0:T(1024)S(1)} %pad_clamp_fusion.2), kind=kCustom, calls=%fused_computation.clone.clone.1 | custom fusion | bytes 8913168 | tf_op jit(solution)/shard_map/while/body/gather | solution.py:49
  230.5 2.2 slice-done.1
  234.3 7.9 %gather_fusion.1 = bf16[68,128,256]{2,1,0:T(8,128)(2,1)} fusion(bf16[80,128,256]{2,1,0:T(8,128)(2,1)} %get-tuple-element.310, s32[1024]{0:T(1024)S(1)} %pad_clamp_fusion.2), kind=kCustom, calls=%fused_computation.1.clone.clone.1 | custom fusion | bytes 8913168 | tf_op jit(solution)/shard_map/while/body/gather | solution.py:48
  244.7 3.0 fusion.59
  247.8 7.9 %gather_fusion = bf16[68,128,256]{2,1,0:T(8,128)(2,1)} fusion(bf16[80,128,256]{2,1,0:T(8,128)(2,1)} %get-tuple-element.309, s32[1024]{0:T(1024)S(1)} %pad_clamp_fusion.2), kind=kCustom, calls=%fused_computation.clone.clone.1 | custom fusion | bytes 8913168 | tf_op jit(solution)/shard_map/while/body/gather | solution.py:49
  261.9 2.2 slice-done.1
  266.7 2.9 convolution_convert_fusion.1
  270.9 4.6 stack.2
  275.4 8.8 %all-to-all-start = ((bf16[32,72,2304]{2,1,0:T(8,128)(2,1)}), bf16[32,72,2304]{2,1,0:T(8,128)(2,1)}, u32[]{:S(2)}, u32[]{:S(2)}) async-start(bf16[32,72,2304]{2,1,0:T(8,128)(2,1)} %stack.2), calls=%async_computation | async-start | bytes 21233664 | tf_op jit(solution)/shard_map/all_to_all | solution.py:125
  284.5 51.9 %all-reduce.3.cloned.1.call-done = bf16[528,2304]{1,0:T(8,128)(2,1)} async-done(((bf16[528,2304]{1,0:T(8,128)(2,1)}), bf16[528,2304]{1,0:T(8,128)(2,1)}) %all-reduce.3.cloned.1.call-update) | async-done | bytes 2433040 | tf_op jit(solution)/shard_map/psum | solution.py:108
  336.4 2.2 fusion.14
  338.6 5.9 multiply_reduce_fusion.1
  344.5 88.9 %all-gather.3.cloned.1.call-done = bf16[2304,2304]{1,0:T(8,128)(2,1)} async-done(((bf16[72,2304]{1,0:T(8,128)(2,1)}), bf16[2304,2304]{1,0:T(8,128)(2,1)}) %all-gather.3.cloned.1.call-update) | async-done | bytes 10616848 | tf_op jit(solution)/shard_map/all_gather | solution.py:115
  433.4 12.3 %fusion.28 = f32[528,2304]{1,0:T(8,128)} fusion(bf16[2304,2304]{1,0:T(8,128)(2,1)} %all-gather.3.cloned.1.call-done, f32[528,2304]{1,0:T(8,128)} %get-tuple-element.163, f32[2304]{0:T(1024)S(1)} %copy-done.5, f32[528]{0:T(1024)S(1)} %add_rsqrt_fusion.1), kind=kOutput, calls=%fused_computation.62 | convolution fusion | flops 5609336832 | bytes 20360256 | tf_op jit(solution)/shard_map/dot_general | solution.py:113
  445.7 54.7 %all-gather.5.cloned.1.call-done = bf16[2304,2304]{1,0:T(8,128)(2,1)} async-done(((bf16[72,2304]{1,0:T(8,128)(2,1)}), bf16[2304,2304]{1,0:T(8,128)(2,1)}) %all-gather.5.cloned.1.call-update) | async-done | bytes 10616848 | tf_op jit(solution)/shard_map/all_gather | solution.py:119
  500.5 12.9 %fusion.24 = bf16[528,2304]{1,0:T(8,128)(2,1)} fusion(bf16[2304,2304]{1,0:T(8,128)(2,1)} %all-gather.5.cloned.1.call-done, f32[528,2304]{1,0:T(8,128)} %fusion.28, f32[528,2304]{1,0:T(8,128)} %get-tuple-element.163, f32[2304]{0:T(1024)S(1)} %copy-done.5, f32[528]{0:T(1024)S(1)} %add_rsqrt_fusion.1), kind=kOutput, calls=%fused_computation.44 | convolution fusion | flops 5621501952 | bytes 22793280 | tf_op jit(solution)/shard_map/dot_general | solution.py:118
  513.4 11.5 %convolution_convert_fusion = bf16[528,2304]{1,0:T(8,128)(2,1)} fusion(bf16[528,2304]{1,0:T(8,128)(2,1)} %fusion.24, bf16[2304,2304]{1,0:T(8,128)(2,1)} %bitcast.5), kind=kOutput, calls=%fused_computation.45 | convolution fusion | flops 5606903808 | bytes 15482880 | tf_op jit(solution)/shard_map/dot_general | solution.py:122
  525.7 62.5 %all-reduce.5.cloned.1.call-done = bf16[528,2304]{1,0:T(8,128)(2,1)} async-done(((bf16[528,2304]{1,0:T(8,128)(2,1)}), bf16[528,2304]{1,0:T(8,128)(2,1)}) %all-reduce.5.cloned.1.call-update) | async-done | bytes 2433040 | tf_op jit(solution)/shard_map/psum | solution.py:132
  588.2 2.2 multiply_reduce_fusion
  590.5 2.2 convert_element_type.45
  592.7 3.2 fusion.25
  (190 shorter events, 91.1 us)
Async XLA Ops:
  7.4 259.3 %copy-start = (bf16[512,2304]{1,0:T(8,128)(2,1)S(1)}, bf16[512,2304]{1,0:T(8,128)(2,1)}, u32[]{:S(2)}) copy-start(bf16[512,2304]{1,0:T(8,128)(2,1)} %param.23) | copy-start | bytes 7077892
  7.4 329.0 %all-reduce.3.cloned.1.call-start = ((), (), s32[]{:S(2)}) async-start(), calls=%async_computation.1 | async-start | bytes 4866048 | tf_op jit(solution)/shard_map/psum | solution.py:108
  38.4 0.7 copy-start.3
  38.4 2.2 slice-start
  41.8 2.2 slice-start.1
  69.8 0.7 copy-start.3
  69.8 2.2 slice-start
  73.3 2.2 slice-start.1
  101.2 0.7 copy-start.3
  101.2 2.2 slice-start
  104.7 2.2 slice-start.1
  132.7 0.7 copy-start.3
  132.7 2.2 slice-start
  136.2 2.2 slice-start.1
  164.1 0.7 copy-start.3
  164.1 2.2 slice-start
  167.6 2.2 slice-start.1
  195.5 0.7 copy-start.3
  195.5 2.2 slice-start
  199.0 2.2 slice-start.1
  227.0 0.7 copy-start.3
  227.0 2.2 slice-start
  230.5 2.2 slice-start.1
  258.4 0.7 copy-start.3
  258.4 2.2 slice-start
  261.9 2.2 slice-start.1
  266.7 4.1 copy-start.2
  269.7 163.7 %all-gather.3.cloned.1.call-start = ((), (), s32[]{:S(2)}) async-start(), calls=%async_computation.2 | async-start | bytes 10948608 | tf_op jit(solution)/shard_map/all_gather | solution.py:115
  270.3 230.2 %all-gather.5.cloned.1.call-start = ((), (), s32[]{:S(2)}) async-start(), calls=%async_computation.3 | async-start | bytes 10948608 | tf_op jit(solution)/shard_map/all_gather | solution.py:119
  275.4 63.2 %copy-start.4 = (f32[2304]{0:T(1024)S(1)}, f32[2304]{0:T(1024)}, u32[]{:S(2)}) copy-start(f32[2304]{0:T(1024)} %param.24) | copy-start | bytes 27652
  275.4 237.9 %all-to-all-start = ((bf16[32,72,2304]{2,1,0:T(8,128)(2,1)}), bf16[32,72,2304]{2,1,0:T(8,128)(2,1)}, u32[]{:S(2)}, u32[]{:S(2)}) async-start(bf16[32,72,2304]{2,1,0:T(8,128)(2,1)} %stack.2), calls=%async_computation | async-start | bytes 21233664 | tf_op jit(solution)/shard_map/all_to_all | solution.py:125
  284.2 304.0 %all-reduce.5.cloned.1.call-start = ((), (), s32[]{:S(2)}) async-start(), calls=%async_computation.4 | async-start | bytes 4866048 | tf_op jit(solution)/shard_map/psum | solution.py:132
  338.6 94.8 %copy-start.5 = (f32[2304]{0:T(1024)S(1)}, f32[2304]{0:T(1024)}, u32[]{:S(2)}) copy-start(f32[2304]{0:T(1024)} %param.25) | copy-start | bytes 27652
  590.4 5.4 copy-start.1
Sparse Core Ops, SparseCore 0:
  269.8 66.5 all-reduce.2
  525.0 63.1 all-reduce.4
Sparse Core Ops, SparseCore 1:
  272.5 160.8 all-gather.2
  435.6 64.8 all-gather.4
